TPU v7x, 256 devices: a whole 4x4x8 slice. The times are simulated.
256 devices in a mesh: ctx: 32 (over z, y_hi, core), head: 8 (over x, y_lo).
Axes of the slice: x: 4, y: 4 (y_hi: 2, y_lo: 2; y = y_hi * 2 + y_lo), z: 8, core: 2. Of those that a mesh axis runs over, the one named last changes fastest.
Arguments:
- queries: bfloat16 [20480, 2048], P('ctx', 'head'), may hold values from -8 to 8
- keys: bfloat16 [20480, 2048], P('ctx', 'head'), may hold values from -6 to 6
- values: bfloat16 [20480, 2048], P('ctx', 'head'), may hold values from -6 to 6
- key_weight: bfloat16 [16, 16, 128], P('head'), may hold values from -1.5 to 1.5
- value_weight: bfloat16 [16, 16, 128], P('head'), may hold values from -1.5 to 1.5
Outputs:
- attended: bfloat16 [20480, 2048], P(('ctx', 'head'))
All inputs are finite; a program needn't handle non-finite values.
Results may differ from a plain program's by a relative error of at most 0.0061.
Values may be sent and summed in bfloat16 or wider, within the bound.
No kernel may reach another device: no remote copies, remote signals or barrier semaphores. Data moves between devices by JAX's collectives and lax.ppermute only.
A program may use at most 64 MiB of HBM per device.

v0:
```python
import math
import jax
import jax.numpy as jnp
from jax import lax
from jax.sharding import PartitionSpec as P

query_span = 512
key_span = 1024


def from_partner(shard, axis, stride):
    return lax.ppermute(shard, axis, [(i, i ^ 1 << stride) for i in range(lax.axis_size(axis))])


def fold_rows(values_in, weight):
    row_count, channels = values_in.shape
    head_count, group_size, head_width = weight.shape
    grouped = values_in.reshape(row_count // group_size, group_size, head_count, head_width)
    folded = jnp.einsum("gjhd,hjd->ghd", grouped, weight, preferred_element_type=jnp.float32)
    return folded.astype(jnp.bfloat16).reshape(row_count // group_size, channels)


def attend(carried, query_heads, key_rows, value_rows):
    top_now, total_now, summed = carried
    query_count, head_count, head_width = query_heads.shape
    key_count = key_rows.shape[0]
    key_heads = key_rows.reshape(key_count, head_count, head_width)
    value_heads = value_rows.reshape(key_count, head_count, head_width)
    score_scale = 1.0 / math.sqrt(head_width)
    top_parts, total_parts, sum_parts = ([], [], [])
    for query_start in range(0, query_count, query_span):
        query_end = min(query_count, query_start + query_span)
        run_top = top_now[:, query_start:query_end]
        run_total = total_now[:, query_start:query_end]
        run_sum = summed[:, query_start:query_end]
        for key_start in range(0, key_count, key_span):
            key_end = min(key_count, key_start + key_span)
            scores = (
                jnp.einsum(
                    "qhd,khd->hqk",
                    query_heads[query_start:query_end],
                    key_heads[key_start:key_end],
                    preferred_element_type=jnp.float32,
                )
                * score_scale
            )
            new_top = jnp.maximum(run_top, jnp.max(scores, axis=2))
            factor = jnp.exp(run_top - new_top)
            weights = jnp.exp(scores - new_top[:, :, None])
            run_total = run_total * factor + jnp.sum(weights, axis=2)
            run_sum = run_sum * factor[:, :, None] + jnp.einsum(
                "hqk,khd->hqd",
                weights.astype(jnp.bfloat16),
                value_heads[key_start:key_end],
                preferred_element_type=jnp.float32,
            )
            run_top = new_top
        top_parts.append(run_top)
        total_parts.append(run_total)
        sum_parts.append(run_sum)
    return (
        jnp.concatenate(top_parts, 1),
        jnp.concatenate(total_parts, 1),
        jnp.concatenate(sum_parts, 1),
    )


def body(queries, keys, values, key_weight, value_weight):
    block_rows, channels = queries.shape
    head_count, group_size, head_width = key_weight.shape
    query_heads = queries.reshape(block_rows, head_count, head_width)
    folded_keys = fold_rows(keys, key_weight)
    folded_values = fold_rows(values, value_weight)
    carried = (
        jnp.full((head_count, block_rows), -jnp.inf, jnp.float32),
        jnp.zeros((head_count, block_rows), jnp.float32),
        jnp.zeros((head_count, block_rows, head_width), jnp.float32),
    )
    carried = attend(carried, query_heads, keys, values)
    bit_count = lax.axis_size("ctx").bit_length() - 1
    for bit_index in range(bit_count):
        far_keys, far_values = from_partner((keys, values), "ctx", bit_index)
        carried = attend(carried, query_heads, far_keys, far_values)
    carried = attend(
        carried,
        query_heads,
        lax.all_gather(folded_keys, "ctx", axis=0, tiled=True),
        lax.all_gather(folded_values, "ctx", axis=0, tiled=True),
    )
    top_now, total_now, summed = carried
    result = (summed / total_now[:, :, None]).astype(jnp.bfloat16)
    result = jnp.transpose(result, (1, 0, 2)).reshape(block_rows, head_count * head_width)
    return lax.all_to_all(result, "head", split_axis=0, concat_axis=1, tiled=True)


def solution(mesh):
    in_specs = (
        P("ctx", "head"),
        P("ctx", "head"),
        P("ctx", "head"),
        P("head", None, None),
        P("head", None, None),
    )
    out_specs = P(("ctx", "head"), None)
    return jax.shard_map(body, mesh=mesh, in_specs=in_specs, out_specs=out_specs, check_vma=False)
```

profile of v0, /device:TPU:16, one launch (start us, length us, event | category | flops | bytes accessed | tf_op | source)
XLA Modules:
  0.0 195.2 jit_solution(15290584683478375523)
XLA Ops:
  0.0 1.9 copy.149
  1.9 7.2 %collective-permute-start.8 = (bf16[640,256]{0,1:T(8,128)(2,1)}, bf16[640,256]{0,1:T(8,128)(2,1)}, u32[]{:S(2)}, u32[]{:S(2)}) collective-permute-start(bf16[640,256]{0,1:T(8,128)(2,1)} %copy.149), channel_id=1, source_target_pairs={{0,128},{8,136},{16,144},{24,152},{32,160},{40,168},{48,176},{56,1... | collective-permute-start | bytes 983048 | tf_op jit(solution)/shard_map/ppermute | solution.py:12
  9.1 1.5 collective-permute-start.6
  10.6 1.0 collective-permute-start.4
  11.6 0.3 collective-permute-start.2
  11.9 1.1 reshape.407
  13.0 0.7 bitcast_convert_fusion.1
  13.7 0.4 multiply_reduce_fusion.7
  14.1 56.2 %all_gather.6 = bf16[1280,256]{1,0:T(8,128)(2,1)S(1)} all-gather(bf16[40,256]{1,0:T(8,128)(2,1)S(1)} %bitcast.164), channel_id=1, replica_groups=mesh['ctx'=32,'head'=8] {'ctx'}, dimensions={0}, use_global_device_ids=true | all-gather | bytes 675840 | tf_op jit(solution)/shard_map/all_gather | solution.py:87
  70.3 0.8 copy-done.4
  71.6 0.4 fusion.173
  72.0 0.9 fusion.168
  73.0 2.7 %bitcast_reduce_fusion = (f32[2,512]{1,0:T(2,128)S(1)}, f32[2,1024,512]{2,1,0:T(8,128)}) fusion(bf16[1024,2,128]{0,2,1:T(8,128)(2,1)S(1)} %bitcast.146, bf16[512,2,128]{0,2,1:T(8,128)(2,1)S(1)} %bitcast.127), kind=kOutput, calls=%fused_computation.1 | convolution fusion | flops 270531584 | bytes 4984832 | tf_op jit(solution)/shard_map/qhd,khd->hqk/dot_general | solution.py:39
  75.8 0.4 fusion.175
  76.1 1.8 reshape.409
  77.9 0.7 bitcast_convert_fusion
  78.6 1.3 multiply_reduce_fusion.6
  80.0 43.2 %all_gather.7 = bf16[1280,256]{1,0:T(8,128)(2,1)} all-gather(bf16[40,256]{1,0:T(8,128)(2,1)S(1)} %bitcast.165), channel_id=1, replica_groups=mesh['ctx'=32,'head'=8] {'ctx'}, dimensions={0}, use_global_device_ids=true | all-gather | bytes 675840 | tf_op jit(solution)/shard_map/all_gather | solution.py:88
  123.2 1.9 fusion.167
  125.1 1.9 copy.152
  126.9 1.9 slice.85
  128.8 2.0 %copy.279 = bf16[1024,256]{0,1:T(8,128)(2,1)} copy(bf16[1024,256]{1,0:T(8,128)(2,1)} %slice.85) | data formatting | bytes 1048576
  130.9 0.8 copy.281
  131.6 0.7 multiply_reduce_fusion.5
  132.6 1.5 collective-permute-start.9
  134.1 1.4 fusion.169
  135.5 1.6 multiply_reduce_fusion
  137.4 1.4 fusion.170
  138.7 1.6 multiply_reduce_fusion.1
  140.4 2.9 %collective-permute-start.5 = (bf16[640,256]{0,1:T(8,128)(2,1)S(1)}, bf16[640,256]{0,1:T(8,128)(2,1)S(1)}, u32[]{:S(2)}, u32[]{:S(2)}) collective-permute-start(bf16[640,256]{0,1:T(8,128)(2,1)S(1)} %copy-done.8), channel_id=1, source_target_pairs={{0,32},{8,40},{16,48},{24,56},{32,0},{40,8},{48,16},{56,24},{64,96... | collective-permute-start | bytes 983048 | tf_op jit(solution)/shard_map/ppermute | solution.py:12
  143.3 1.4 fusion.171
  144.7 1.6 multiply_reduce_fusion.2
  146.3 1.2 collective-permute-start.3
  147.5 1.4 fusion.172
  148.8 1.6 multiply_reduce_fusion.3
  150.6 1.6 multiply_reduce_fusion.4
  152.2 1.4 fusion.174
  153.6 1.3 fusion.3
  155.0 1.3 fusion.9
  156.3 9.2 %collective-permute-done.7 = bf16[640,256]{0,1:T(8,128)(2,1)S(1)} collective-permute-done((bf16[640,256]{0,1:T(8,128)(2,1)S(1)}, bf16[640,256]{0,1:T(8,128)(2,1)S(1)}, u32[]{:S(2)}, u32[]{:S(2)}) %collective-permute-start.7) | collective-permute-done | bytes 327712 | tf_op jit(solution)/shard_map/ppermute | solution.py:12
  165.5 0.3 fusion.129
  165.8 0.7 fusion.23
  166.6 0.3 fusion.131
  166.9 0.4 fusion.115
  167.2 0.7 fusion.25
  168.0 0.7 fusion.21
  168.9 0.4 fusion.123
  169.2 0.3 fusion.127
  169.5 0.4 fusion.109
  170.1 0.4 fusion.121
  170.4 1.0 copy-done
  171.5 1.1 fusion.15
  172.9 0.7 fusion.1
  173.6 0.7 fusion.27
  174.3 1.3 fusion.5
  175.7 0.3 fusion.133
  176.0 0.4 fusion.111
  176.4 0.5 fusion.93
  177.0 0.9 fusion.48
  177.9 1.5 fusion.87
  179.4 0.4 fusion.103
  180.0 0.3 copy.213
  180.6 13.9 %all_to_all.19 = bf16[8,80,256]{2,1,0:T(8,128)(2,1)S(1)} all-to-all(bf16[8,80,256]{2,1,0:T(8,128)(2,1)S(1)} %all_to_all.14), channel_id=1, replica_groups=mesh['ctx'=32,'head'=8] {'head'}, dimensions={0} | all-to-all | bytes 655360 | tf_op jit(solution)/shard_map/all_to_all | solution.py:93
  194.5 0.8 copy.289
  (58 shorter events, 2.6 us)
Async XLA Ops:
  0.0 71.1 %slice-start.2 = ((bf16[640,256]{1,0:T(8,128)(2,1)}), bf16[512,256]{1,0:T(8,128)(2,1)S(1)}, s32[]{:S(2)}) async-start(bf16[640,256]{1,0:T(8,128)(2,1)} %param.5), calls=%async_computation.3 | async-start | bytes 524288 | tf_op jit(solution)/shard_map/slice | solution.py:41
  1.9 69.6 %slice-start.3 = ((bf16[640,256]{1,0:T(8,128)(2,1)}), bf16[128,256]{1,0:T(8,128)(2,1)S(1)}, s32[]{:S(2)}) async-start(bf16[640,256]{1,0:T(8,128)(2,1)} %param.5), calls=%async_computation.4 | async-start | bytes 131072 | tf_op jit(solution)/shard_map/slice | solution.py:41
  1.9 69.7 %copy-start.1 = (bf16[640,256]{1,0:T(8,128)(2,1)S(1)}, bf16[640,256]{1,0:T(8,128)(2,1)}, u32[]{:S(2)}) copy-start(bf16[640,256]{1,0:T(8,128)(2,1)} %param.6) | copy-start | bytes 983044
  1.9 130.4 %collective-permute-start.8 = (bf16[640,256]{0,1:T(8,128)(2,1)}, bf16[640,256]{0,1:T(8,128)(2,1)}, u32[]{:S(2)}, u32[]{:S(2)}) collective-permute-start(bf16[640,256]{0,1:T(8,128)(2,1)} %copy.149), channel_id=1, source_target_pairs={{0,128},{8,136},{16,144},{24,152},{32,160},{40,168},{48,176},{56,1... | collective-permute-start | bytes 983048 | tf_op jit(solution)/shard_map/ppermute | solution.py:12
  9.1 128.0 %collective-permute-start.6 = (bf16[640,256]{0,1:T(8,128)(2,1)}, bf16[640,256]{0,1:T(8,128)(2,1)}, u32[]{:S(2)}, u32[]{:S(2)}) collective-permute-start(bf16[640,256]{0,1:T(8,128)(2,1)} %copy.149), channel_id=1, source_target_pairs={{0,64},{8,72},{16,80},{24,88},{32,96},{40,104},{48,112},{56,120},{... | collective-permute-start | bytes 983048 | tf_op jit(solution)/shard_map/ppermute | solution.py:12
  10.6 129.8 %collective-permute-start.4 = (bf16[640,256]{0,1:T(8,128)(2,1)}, bf16[640,256]{0,1:T(8,128)(2,1)}, u32[]{:S(2)}, u32[]{:S(2)}) collective-permute-start(bf16[640,256]{0,1:T(8,128)(2,1)} %copy.149), channel_id=1, source_target_pairs={{0,32},{8,40},{16,48},{24,56},{32,0},{40,8},{48,16},{56,24},{64,96... | collective-permute-start | bytes 983048 | tf_op jit(solution)/shard_map/ppermute | solution.py:12
  11.6 134.7 %collective-permute-start.2 = (bf16[640,256]{0,1:T(8,128)(2,1)}, bf16[640,256]{0,1:T(8,128)(2,1)}, u32[]{:S(2)}, u32[]{:S(2)}) collective-permute-start(bf16[640,256]{0,1:T(8,128)(2,1)} %copy.149), channel_id=1, source_target_pairs={{0,16},{8,24},{16,0},{24,8},{32,48},{40,56},{48,32},{56,40},{64,80... | collective-permute-start | bytes 983048 | tf_op jit(solution)/shard_map/ppermute | solution.py:12
  11.9 138.5 %collective-permute-start = (bf16[640,256]{0,1:T(8,128)(2,1)}, bf16[640,256]{0,1:T(8,128)(2,1)}, u32[]{:S(2)}, u32[]{:S(2)}) collective-permute-start(bf16[640,256]{0,1:T(8,128)(2,1)} %copy.149), channel_id=1, source_target_pairs={{0,8},{8,0},{16,24},{24,16},{32,40},{40,32},{48,56},{56,48},{64,72... | collective-permute-start | bytes 983048 | tf_op jit(solution)/shard_map/ppermute | solution.py:12
  70.3 0.8 copy-start.4
  73.0 2.7 %slice-start.1 = ((bf16[1280,256]{1,0:T(8,128)(2,1)}), bf16[256,256]{1,0:T(8,128)(2,1)S(1)}, s32[]{:S(2)}) async-start(bf16[1280,256]{1,0:T(8,128)(2,1)} %copy-done.4), calls=%async_computation.2 | async-start | bytes 262144 | tf_op jit(solution)/shard_map/slice | solution.py:42
  75.7 4.2 %copy-start.6 = (bf16[256,256]{0,1:T(8,128)(2,1)}, bf16[256,256]{0,1:T(8,128)(2,1)S(1)}, u32[]{:S(2)}) copy-start(bf16[256,256]{0,1:T(8,128)(2,1)S(1)} %copy.280) | copy-start | bytes 393220
  123.2 7.7 %slice-start = ((bf16[1280,256]{1,0:T(8,128)(2,1)}), bf16[256,256]{1,0:T(8,128)(2,1)S(1)}, s32[]{:S(2)}) async-start(bf16[1280,256]{1,0:T(8,128)(2,1)} %all_gather.7), calls=%async_computation.1 | async-start | bytes 262144 | tf_op jit(solution)/shard_map/slice | solution.py:54
  131.6 1.0 copy-start.8
  132.6 35.3 %collective-permute-start.9 = (bf16[640,256]{0,1:T(8,128)(2,1)S(1)}, bf16[640,256]{0,1:T(8,128)(2,1)S(1)}, u32[]{:S(2)}, u32[]{:S(2)}) collective-permute-start(bf16[640,256]{0,1:T(8,128)(2,1)S(1)} %copy-done.8), channel_id=1, source_target_pairs={{0,128},{8,136},{16,144},{24,152},{32,160},{40,168},{48,176},{56,1... | collective-permute-start | bytes 983048 | tf_op jit(solution)/shard_map/ppermute | solution.py:12
  137.1 28.4 %collective-permute-start.7 = (bf16[640,256]{0,1:T(8,128)(2,1)S(1)}, bf16[640,256]{0,1:T(8,128)(2,1)S(1)}, u32[]{:S(2)}, u32[]{:S(2)}) collective-permute-start(bf16[640,256]{0,1:T(8,128)(2,1)S(1)} %copy-done.8), channel_id=1, source_target_pairs={{0,64},{8,72},{16,80},{24,88},{32,96},{40,104},{48,112},{56,120},{... | collective-permute-start | bytes 983048 | tf_op jit(solution)/shard_map/ppermute | solution.py:12
  140.4 26.2 %collective-permute-start.5 = (bf16[640,256]{0,1:T(8,128)(2,1)S(1)}, bf16[640,256]{0,1:T(8,128)(2,1)S(1)}, u32[]{:S(2)}, u32[]{:S(2)}) collective-permute-start(bf16[640,256]{0,1:T(8,128)(2,1)S(1)} %copy-done.8), channel_id=1, source_target_pairs={{0,32},{8,40},{16,48},{24,56},{32,0},{40,8},{48,16},{56,24},{64,96... | collective-permute-start | bytes 983048 | tf_op jit(solution)/shard_map/ppermute | solution.py:12
  146.3 27.3 %collective-permute-start.3 = (bf16[640,256]{0,1:T(8,128)(2,1)S(1)}, bf16[640,256]{0,1:T(8,128)(2,1)S(1)}, u32[]{:S(2)}, u32[]{:S(2)}) collective-permute-start(bf16[640,256]{0,1:T(8,128)(2,1)S(1)} %copy-done.8), channel_id=1, source_target_pairs={{0,16},{8,24},{16,0},{24,8},{32,48},{40,56},{48,32},{56,40},{64,80... | collective-permute-start | bytes 983048 | tf_op jit(solution)/shard_map/ppermute | solution.py:12
  150.5 27.4 %collective-permute-start.1 = (bf16[640,256]{0,1:T(8,128)(2,1)S(1)}, bf16[640,256]{0,1:T(8,128)(2,1)S(1)}, u32[]{:S(2)}, u32[]{:S(2)}) collective-permute-start(bf16[640,256]{0,1:T(8,128)(2,1)S(1)} %copy-done.8), channel_id=1, source_target_pairs={{0,8},{8,0},{16,24},{24,16},{32,40},{40,32},{48,56},{56,48},{64,72... | collective-permute-start | bytes 983048 | tf_op jit(solution)/shard_map/ppermute | solution.py:12
  153.6 1.4 copy-start.9
  167.9 0.9 copy-start.7
  168.8 1.2 copy-start.2
  169.2 2.2 %copy-start = (f32[2,1024,512]{2,1,0:T(8,128)S(1)}, f32[2,1024,512]{2,1,0:T(8,128)}, u32[]{:S(2)}) copy-start(f32[2,1024,512]{2,1,0:T(8,128)} %get-tuple-element.56) | copy-start | bytes 12582916
  171.5 1.2 copy-start.5
  174.3 2.1 %copy-start.3 = (bf16[640,256]{1,0:T(8,128)(2,1)S(1)}, bf16[640,256]{1,0:T(8,128)(2,1)}, u32[]{:S(2)}) copy-start(bf16[640,256]{1,0:T(8,128)(2,1)} %param.7) | copy-start | bytes 983044
where the time goes:
time: 196 us; the launch traced here: 195 us
  blocking collectives  113 us (58%)
  matrix products  31.2 us (16%)
  starting transfers between devices  16 us (8%)
  local copies, waits for them, and re-layouts  15.4 us (8%)
  other arithmetic  9.62 us (5%)
  waiting for transfers between devices  9.24 us (5%)
    all_gather x1, blocking collectives, body(): lax.all_gather(folded_keys, 'ctx', axis=0, tiled=True)  56.2 us
    all_gather x1, blocking collectives, body(): lax.all_gather(folded_values, 'ctx', axis=0, tiled=True)  43.2 us
    dot_general x16, matrix products, attend(): jnp.einsum('qhd,khd->hqk', query_heads[query_start:query_end], key_heads[...  21.8 us
    ppermute x10, starting transfers between devices, from_partner(): lax.ppermute(shard, axis, [(i, i ^ 1 << stride) for i in range(lax.axis_s...  16 us
    all_to_all x1, blocking collectives, body(): lax.all_to_all(result, 'head', split_axis=0, concat_axis=1, tiled=True)  13.9 us
    dot_general x16, matrix products, attend(): jnp.einsum('hqk,khd->hqd', weights.astype(jnp.bfloat16), value_heads[key_...  9.46 us
    unnamed x32, local copies, waits for them, and re-layouts  9.32 us
    ppermute x10, waiting for transfers between devices, from_partner(): lax.ppermute(shard, axis, [(i, i ^ 1 << stride) for i in range(lax.axis_s...  9.24 us
  transfers between devices with their start and end apart: 10, of which 1 were waited for; matrix products, arithmetic and copies ran while one was open for 25% of the time, Pallas kernels for 0%

commit v1 on v0

--- a/solution.py
+++ b/solution.py
@@ -85,7 +85,9 @@
         carried,
         query_heads,
         lax.all_gather(folded_keys, "ctx", axis=0, tiled=True),
-        lax.all_gather(folded_values, "ctx", axis=0, tiled=True),
+        jnp.concatenate(
+            lax.all_to_all(jnp.stack([folded_values] * lax.axis_size("ctx")), "ctx", 0, 0), axis=0
+        ),
     )
     top_now, total_now, summed = carried
     result = (summed / total_now[:, :, None]).astype(jnp.bfloat16)

time: 196 us -> 177 us (0.903)
  blocking collectives: 113 us -> 74.2 us
  matrix products: 31.2 us -> 42.2 us
  starting transfers between devices: 16 us -> 23.7 us
  local copies, waits for them, and re-layouts: 15.4 us -> 13.1 us
  waiting for transfers between devices: 9.24 us -> 11.5 us
    all_gather x1 -> x0, blocking collectives: 43.2 us -> none  [body(): lax.all_gather(folded_values, 'ctx', axis=0, tiled=True)]
    dot_general x16, matrix products: 9.46 us -> 21.6 us  [attend(): jnp.einsum('hqk,khd->hqd', weights.astype(jnp.bfloat16), value_heads[key_...]
    all_to_all x0 -> x1, starting transfers between devices: none -> 7.53 us  [body(): lax.all_to_all(jnp.stack([folded_values] * lax.axis_size('ctx')), 'ctx',...]
    all_gather x1, blocking collectives: 56.2 us -> 61.3 us  [body(): lax.all_gather(folded_keys, 'ctx', axis=0, tiled=True)]
    unnamed x32 -> x94, local copies, waits for them, and re-layouts: 9.32 us -> 4.61 us
    another operation x0 -> x2, local copies, waits for them, and re-layouts: none -> 3.41 us  [the longest x1 2.52 us: attend(): value_heads = value_rows.reshape(key_count, head_count, head_width)]
    ppermute x10, waiting for transfers between devices: 9.24 us -> 11.5 us  [from_partner(): lax.ppermute(shard, axis, [(i, i ^ 1 << stride) for i in range(lax.axis_s...]
  transfers between devices with their start and end apart: 10 -> 11, of which waited for: 1 -> 2; matrix products, arithmetic and copies ran while one was open for 25% -> 32% of each run, Pallas kernels for 0% -> 0%
where the time goes in v1:
time: 177 us; the launch traced here: 175 us
  blocking collectives  74.2 us (42%)
  matrix products  42.2 us (24%)
  starting transfers between devices  23.7 us (13%)
  local copies, waits for them, and re-layouts  13.1 us (7%)
  waiting for transfers between devices  11.5 us (6%)
  other arithmetic  9.69 us (5%)
    all_gather x1, blocking collectives, body(): lax.all_gather(folded_keys, 'ctx', axis=0, tiled=True)  61.3 us
    dot_general x16, matrix products, attend(): jnp.einsum('hqk,khd->hqd', weights.astype(jnp.bfloat16), value_heads[key_...  21.6 us
    dot_general x16, matrix products, attend(): jnp.einsum('qhd,khd->hqk', query_heads[query_start:query_end], key_heads[...  20.6 us
    ppermute x10, starting transfers between devices, from_partner(): lax.ppermute(shard, axis, [(i, i ^ 1 << stride) for i in range(lax.axis_s...  16.2 us
    all_to_all x1, blocking collectives, body(): lax.all_to_all(result, 'head', split_axis=0, concat_axis=1, tiled=True)  12.9 us
    ppermute x10, waiting for transfers between devices, from_partner(): lax.ppermute(shard, axis, [(i, i ^ 1 << stride) for i in range(lax.axis_s...  11.5 us
    all_to_all x1, starting transfers between devices, body(): lax.all_to_all(jnp.stack([folded_values] * lax.axis_size('ctx')), 'ctx',...  7.53 us
    reduce_sum x10, other arithmetic, attend(): run_total = run_total * factor + jnp.sum(weights, axis=2)  6.15 us
  transfers between devices with their start and end apart: 11, of which 2 were waited for; matrix products, arithmetic and copies ran while one was open for 32% of the time, Pallas kernels for 0%

profile of v1, /device:TPU:16, one launch (start us, length us, event | category | flops | bytes accessed | tf_op | source)
XLA Modules:
  0.0 175.2 jit_solution(4421675616270305893)
XLA Ops:
  0.0 1.9 %copy.146 = bf16[640,256]{0,1:T(8,128)(2,1)} copy(bf16[640,256]{1,0:T(8,128)(2,1)} %param.6) | data formatting | bytes 655360 | tf_op args[1]
  1.9 7.2 %collective-permute-start.8 = (bf16[640,256]{0,1:T(8,128)(2,1)}, bf16[640,256]{0,1:T(8,128)(2,1)}, u32[]{:S(2)}, u32[]{:S(2)}) collective-permute-start(bf16[640,256]{0,1:T(8,128)(2,1)} %copy.146), channel_id=1, source_target_pairs={{0,128},{8,136},{16,144},{24,152},{32,160},{40,168},{48,176},{56,1... | collective-permute-start | bytes 983048 | tf_op jit(solution)/shard_map/ppermute | solution.py:12
  9.1 1.5 collective-permute-start.6
  10.6 1.0 collective-permute-start.4
  12.0 1.1 reshape.405
  13.0 0.7 bitcast_convert_fusion
  13.7 0.4 multiply_reduce_fusion.6
  14.1 0.9 stack.3
  15.0 7.5 %all-to-all-start = ((bf16[32,40,256]{2,1,0:T(8,128)(2,1)}), bf16[32,40,256]{2,1,0:T(8,128)(2,1)}, u32[]{:S(2)}, u32[]{:S(2)}) async-start(bf16[32,40,256]{2,1,0:T(8,128)(2,1)} %stack.3), calls=%async_computation | async-start | bytes 1310720 | tf_op jit(solution)/shard_map/all_to_all | solution.py:89
  22.7 0.4 multiply_reduce_fusion.7
  23.1 61.3 %all_gather.3 = bf16[1280,256]{1,0:T(8,128)(2,1)S(1)} all-gather(bf16[40,256]{1,0:T(8,128)(2,1)S(1)} %bitcast.157), channel_id=1, replica_groups=mesh['ctx'=32,'head'=8] {'ctx'}, dimensions={0}, use_global_device_ids=true | all-gather | bytes 675840 | tf_op jit(solution)/shard_map/all_gather | solution.py:87
  84.9 0.4 fusion.177
  85.3 1.3 fusion.172
  86.7 3.3 %bitcast_reduce_fusion = (f32[2,512]{1,0:T(2,128)}, f32[2,1024,512]{2,1,0:T(8,128)}) fusion(bf16[1024,2,128]{0,2,1:T(8,128)(2,1)S(1)} %bitcast.138, bf16[512,2,128]{0,2,1:T(8,128)(2,1)S(1)} %bitcast.121), kind=kOutput, calls=%fused_computation.1 | convolution fusion | flops 270531584 | bytes 4984832 | tf_op jit(solution)/shard_map/qhd,khd->hqk/dot_general | solution.py:39
  90.0 1.9 %fusion.179 = (f32[2,512]{1,0:T(2,128)}, f32[2,512,256]{1,2,0:T(8,128)}) fusion(bf16[256,2,128]{0,2,1:T(8,128)(2,1)S(1)} %bitcast.152, bf16[512,2,128]{0,2,1:T(8,128)(2,1)S(1)} %bitcast.122), kind=kOutput, calls=%fused_computation.193 | convolution fusion | flops 67632128 | bytes 1445888 | tf_op jit(solution)/shard_map/qhd,khd->hqk/dot_general | solution.py:39
  92.0 1.0 fusion.171
  93.0 0.9 copy.149
  93.9 0.7 multiply_reduce_fusion.5
  94.5 3.8 %collective-permute-start.9 = (bf16[640,256]{0,1:T(8,128)(2,1)}, bf16[640,256]{0,1:T(8,128)(2,1)S(1)}, u32[]{:S(2)}, u32[]{:S(2)}) collective-permute-start(bf16[640,256]{0,1:T(8,128)(2,1)} %copy.149), channel_id=1, source_target_pairs={{0,128},{8,136},{16,144},{24,152},{32,160},{40,168},{48,176},{56,1... | collective-permute-start | bytes 983048 | tf_op jit(solution)/shard_map/ppermute | solution.py:12
  98.4 1.4 fusion.173
  99.7 1.6 multiply_reduce_fusion
  101.5 1.4 fusion.174
  102.8 1.6 multiply_reduce_fusion.1
  104.4 0.7 collective-permute-start.5
  105.2 1.4 fusion.175
  106.5 1.6 multiply_reduce_fusion.2
  108.2 1.4 collective-permute-start.3
  109.6 0.4 fusion.176
  110.0 0.7 multiply_reduce_fusion.3
  110.7 0.6 copy-done.15
  111.4 1.4 fusion.178
  112.9 0.4 fusion.109
  113.2 0.7 multiply_reduce_fusion.4
  113.9 1.1 collective-permute-done.9
  114.9 1.0 fusion.129
  115.9 1.3 fusion.3
  117.3 10.4 %collective-permute-done.7 = bf16[640,256]{0,1:T(8,128)(2,1)S(1)} collective-permute-done((bf16[640,256]{0,1:T(8,128)(2,1)}, bf16[640,256]{0,1:T(8,128)(2,1)S(1)}, u32[]{:S(2)}, u32[]{:S(2)}) %collective-permute-start.7) | collective-permute-done | bytes 327712 | tf_op jit(solution)/shard_map/ppermute | solution.py:12
  127.7 1.0 fusion.131
  129.0 1.5 fusion.21
  130.6 1.0 fusion.133
  131.8 0.7 fusion.1
  132.5 1.0 fusion.135
  133.5 0.3 fusion.111
  134.1 0.6 multiply_add_fusion.1
  134.7 1.0 fusion.93
  135.7 1.3 fusion.5
  137.0 1.3 fusion.9
  138.3 0.6 multiply_add_fusion
  139.0 0.6 pad_maximum_fusion
  139.6 1.5 fusion.23
  141.1 1.6 fusion.25
  142.6 1.5 fusion.27
  144.1 1.6 fusion.48
  145.7 2.5 %reshape_reshape.3 = bf16[1280,2,128]{2,1,0:T(2,128)(2,1)} reshape(bf16[32,40,256]{2,1,0:T(8,128)(2,1)} %all-to-all-done) | data formatting | bytes 1310720 | tf_op jit(solution)/shard_map/reshape;reshape | solution.py:28
  148.2 1.6 slice.77
  149.8 1.0 slice.79
  150.8 1.6 fusion.123
  152.3 0.9 fusion.157
  153.2 1.6 fusion.121
  154.9 1.2 fusion.15
  156.7 2.5 %fusion.87 = f32[2,512,128]{2,1,0:T(8,128)S(1)} fusion(f32[2,512,128]{2,1,0:T(8,128)S(1)} %fusion.123, f32[2,512,128]{2,1,0:T(8,128)S(1)} %fusion.15, f32[2,512,128]{2,1,0:T(8,128)S(1)} %copy-done.11, f32[2,512,128]{2,1,0:T(8,128)S(1)} %copy-done.12, f32[2,512,128]{2,1,0:T(8,128)S(1)} %copy-done.13, f32[2,512,128]{2,1,0:T(8,128)S(1)} %copy-done.14, ...), kind=kOutput, calls=%fused_computation.74 | convolution fusion | flops 171442176 | bytes 7172096 | tf_op jit(solution)/shard_map/hqk,khd->hqd/dot_general | solution.py:51
  159.3 1.4 fusion.103
  161.5 12.9 %all_to_all.24 = bf16[8,80,256]{2,1,0:T(8,128)(2,1)S(1)} all-to-all(bf16[8,80,256]{2,1,0:T(8,128)(2,1)S(1)} %all_to_all.18), channel_id=1, replica_groups=mesh['ctx'=32,'head'=8] {'head'}, dimensions={0} | all-to-all | bytes 655360 | tf_op jit(solution)/shard_map/all_to_all | solution.py:95
  174.4 0.8 copy.278
  (122 shorter events, 3.4 us)
Async XLA Ops:
  0.0 22.5 %copy-start.6 = (bf16[640,256]{1,0:T(8,128)(2,1)S(1)}, bf16[640,256]{1,0:T(8,128)(2,1)}, u32[]{:S(2)}) copy-start(bf16[640,256]{1,0:T(8,128)(2,1)} %param.6) | copy-start | bytes 983044
  0.0 22.6 %copy-start.35 = (bf16[2,16,128]{2,1,0:T(8,128)(2,1)S(1)}, bf16[2,16,128]{2,1,0:T(8,128)(2,1)}, u32[]{:S(2)}) copy-start(bf16[2,16,128]{2,1,0:T(8,128)(2,1)} %param.8) | copy-start | bytes 24580
  1.9 92.6 %collective-permute-start.8 = (bf16[640,256]{0,1:T(8,128)(2,1)}, bf16[640,256]{0,1:T(8,128)(2,1)}, u32[]{:S(2)}, u32[]{:S(2)}) collective-permute-start(bf16[640,256]{0,1:T(8,128)(2,1)} %copy.146), channel_id=1, source_target_pairs={{0,128},{8,136},{16,144},{24,152},{32,160},{40,168},{48,176},{56,1... | collective-permute-start | bytes 983048 | tf_op jit(solution)/shard_map/ppermute | solution.py:12
  9.1 92.2 %collective-permute-start.6 = (bf16[640,256]{0,1:T(8,128)(2,1)}, bf16[640,256]{0,1:T(8,128)(2,1)}, u32[]{:S(2)}, u32[]{:S(2)}) collective-permute-start(bf16[640,256]{0,1:T(8,128)(2,1)} %copy.146), channel_id=1, source_target_pairs={{0,64},{8,72},{16,80},{24,88},{32,96},{40,104},{48,112},{56,120},{... | collective-permute-start | bytes 983048 | tf_op jit(solution)/shard_map/ppermute | solution.py:12
  10.6 93.8 %collective-permute-start.4 = (bf16[640,256]{0,1:T(8,128)(2,1)}, bf16[640,256]{0,1:T(8,128)(2,1)}, u32[]{:S(2)}, u32[]{:S(2)}) collective-permute-start(bf16[640,256]{0,1:T(8,128)(2,1)} %copy.146), channel_id=1, source_target_pairs={{0,32},{8,40},{16,48},{24,56},{32,0},{40,8},{48,16},{56,24},{64,96... | collective-permute-start | bytes 983048 | tf_op jit(solution)/shard_map/ppermute | solution.py:12
  11.6 96.5 %collective-permute-start.2 = (bf16[640,256]{0,1:T(8,128)(2,1)}, bf16[640,256]{0,1:T(8,128)(2,1)S(1)}, u32[]{:S(2)}, u32[]{:S(2)}) collective-permute-start(bf16[640,256]{0,1:T(8,128)(2,1)} %copy.146), channel_id=1, source_target_pairs={{0,16},{8,24},{16,0},{24,8},{32,48},{40,56},{48,32},{56,40},{64,80... | collective-permute-start | bytes 983048 | tf_op jit(solution)/shard_map/ppermute | solution.py:12
  12.0 98.7 %collective-permute-start = (bf16[640,256]{0,1:T(8,128)(2,1)}, bf16[640,256]{0,1:T(8,128)(2,1)S(1)}, u32[]{:S(2)}, u32[]{:S(2)}) collective-permute-start(bf16[640,256]{0,1:T(8,128)(2,1)} %copy.146), channel_id=1, source_target_pairs={{0,8},{8,0},{16,24},{24,16},{32,40},{40,32},{48,56},{56,48},{64,72... | collective-permute-start | bytes 983048 | tf_op jit(solution)/shard_map/ppermute | solution.py:12
  15.0 69.4 %slice-start.1 = ((bf16[640,256]{1,0:T(8,128)(2,1)}), bf16[512,256]{1,0:T(8,128)(2,1)S(1)}, s32[]{:S(2)}) async-start(bf16[640,256]{1,0:T(8,128)(2,1)} %param.5), calls=%async_computation.3 | async-start | bytes 524288 | tf_op jit(solution)/shard_map/slice | solution.py:41
  15.0 130.7 %all-to-all-start = ((bf16[32,40,256]{2,1,0:T(8,128)(2,1)}), bf16[32,40,256]{2,1,0:T(8,128)(2,1)}, u32[]{:S(2)}, u32[]{:S(2)}) async-start(bf16[32,40,256]{2,1,0:T(8,128)(2,1)} %stack.3), calls=%async_computation | async-start | bytes 1310720 | tf_op jit(solution)/shard_map/all_to_all | solution.py:89
  22.5 62.3 %slice-start.2 = ((bf16[640,256]{1,0:T(8,128)(2,1)}), bf16[128,256]{1,0:T(8,128)(2,1)S(1)}, s32[]{:S(2)}) async-start(bf16[640,256]{1,0:T(8,128)(2,1)} %param.5), calls=%async_computation.4 | async-start | bytes 131072 | tf_op jit(solution)/shard_map/slice | solution.py:41
  84.4 2.3 %copy-start.9 = (bf16[1280,256]{1,0:T(8,128)(2,1)}, bf16[1280,256]{1,0:T(8,128)(2,1)S(1)}, u32[]{:S(2)}) copy-start(bf16[1280,256]{1,0:T(8,128)(2,1)S(1)} %all_gather.3) | copy-start | bytes 1966084
  85.3 27.5 %copy-start.4 = (f32[2,128,640]{2,1,0:T(8,128)}, f32[2,128,640]{2,1,0:T(8,128)S(1)}, u32[]{:S(2)}) copy-start(f32[2,128,640]{2,1,0:T(8,128)S(1)} %get-tuple-element.50) | copy-start | bytes 1966084
  86.7 3.3 %slice-start = ((bf16[1280,256]{1,0:T(8,128)(2,1)}), bf16[256,256]{1,0:T(8,128)(2,1)S(1)}, s32[]{:S(2)}) async-start(bf16[1280,256]{1,0:T(8,128)(2,1)} %copy-done.9), calls=%async_computation.2 | async-start | bytes 262144 | tf_op jit(solution)/shard_map/slice | solution.py:42
  86.7 6.3 %copy-start.7 = (bf16[640,256]{1,0:T(8,128)(2,1)S(1)}, bf16[640,256]{1,0:T(8,128)(2,1)}, u32[]{:S(2)}) copy-start(bf16[640,256]{1,0:T(8,128)(2,1)} %param.7) | copy-start | bytes 983044
  94.5 20.4 %collective-permute-start.9 = (bf16[640,256]{0,1:T(8,128)(2,1)}, bf16[640,256]{0,1:T(8,128)(2,1)S(1)}, u32[]{:S(2)}, u32[]{:S(2)}) collective-permute-start(bf16[640,256]{0,1:T(8,128)(2,1)} %copy.149), channel_id=1, source_target_pairs={{0,128},{8,136},{16,144},{24,152},{32,160},{40,168},{48,176},{56,1... | collective-permute-start | bytes 983048 | tf_op jit(solution)/shard_map/ppermute | solution.py:12
  101.4 26.4 %collective-permute-start.7 = (bf16[640,256]{0,1:T(8,128)(2,1)}, bf16[640,256]{0,1:T(8,128)(2,1)S(1)}, u32[]{:S(2)}, u32[]{:S(2)}) collective-permute-start(bf16[640,256]{0,1:T(8,128)(2,1)} %copy.149), channel_id=1, source_target_pairs={{0,64},{8,72},{16,80},{24,88},{32,96},{40,104},{48,112},{56,120},{... | collective-permute-start | bytes 983048 | tf_op jit(solution)/shard_map/ppermute | solution.py:12
  104.4 26.1 %collective-permute-start.5 = (bf16[640,256]{0,1:T(8,128)(2,1)}, bf16[640,256]{0,1:T(8,128)(2,1)S(1)}, u32[]{:S(2)}, u32[]{:S(2)}) collective-permute-start(bf16[640,256]{0,1:T(8,128)(2,1)} %copy.149), channel_id=1, source_target_pairs={{0,32},{8,40},{16,48},{24,56},{32,0},{40,8},{48,16},{56,24},{64,96... | collective-permute-start | bytes 983048 | tf_op jit(solution)/shard_map/ppermute | solution.py:12
  108.2 24.3 %collective-permute-start.3 = (bf16[640,256]{0,1:T(8,128)(2,1)}, bf16[640,256]{0,1:T(8,128)(2,1)S(1)}, u32[]{:S(2)}, u32[]{:S(2)}) collective-permute-start(bf16[640,256]{0,1:T(8,128)(2,1)} %copy.149), channel_id=1, source_target_pairs={{0,16},{8,24},{16,0},{24,8},{32,48},{40,56},{48,32},{56,40},{64,80... | collective-permute-start | bytes 983048 | tf_op jit(solution)/shard_map/ppermute | solution.py:12
  110.6 0.7 copy-start.15
  110.6 45.5 %collective-permute-start.1 = (bf16[640,256]{0,1:T(8,128)(2,1)}, bf16[640,256]{0,1:T(8,128)(2,1)}, u32[]{:S(2)}, u32[]{:S(2)}) collective-permute-start(bf16[640,256]{0,1:T(8,128)(2,1)} %copy.149), channel_id=1, source_target_pairs={{0,8},{8,0},{16,24},{24,16},{32,40},{40,32},{48,56},{56,48},{64,72... | collective-permute-start | bytes 983048 | tf_op jit(solution)/shard_map/ppermute | solution.py:12
  111.4 1.9 %copy-start.16 = (bf16[640,256]{0,1:T(8,128)(2,1)S(1)}, bf16[640,256]{0,1:T(8,128)(2,1)}, u32[]{:S(2)}) copy-start(bf16[640,256]{0,1:T(8,128)(2,1)} %copy-done.15) | copy-start | bytes 983044
  112.8 21.3 %copy-start.29 = (f32[2,128]{1,0:T(2,128)}, f32[2,128]{1,0:T(2,128)S(1)}, u32[]{:S(2)}) copy-start(f32[2,128]{1,0:T(2,128)S(1)} %get-tuple-element.34) | copy-start | bytes 3076
  112.8 21.3 %copy-start.31 = (f32[2,128]{1,0:T(2,128)}, f32[2,128]{1,0:T(2,128)S(1)}, u32[]{:S(2)}) copy-start(f32[2,128]{1,0:T(2,128)S(1)} %get-tuple-element.28) | copy-start | bytes 3076
  112.8 21.3 %copy-start.33 = (f32[2,128]{1,0:T(2,128)}, f32[2,128]{1,0:T(2,128)S(1)}, u32[]{:S(2)}) copy-start(f32[2,128]{1,0:T(2,128)S(1)} %get-tuple-element.29) | copy-start | bytes 3076
  112.8 3.1 %copy-start.32 = (f32[2,512]{1,0:T(2,128)S(1)}, f32[2,512]{1,0:T(2,128)}, u32[]{:S(2)}) copy-start(f32[2,512]{1,0:T(2,128)} %get-tuple-element.53) | copy-start | bytes 12292
  112.9 3.1 %copy-start.34 = (f32[2,512]{1,0:T(2,128)S(1)}, f32[2,512]{1,0:T(2,128)}, u32[]{:S(2)}) copy-start(f32[2,512]{1,0:T(2,128)} %get-tuple-element.55) | copy-start | bytes 12292
  128.7 2.9 %copy-start.3 = (f32[2,512,256]{1,2,0:T(8,128)S(1)}, f32[2,512,256]{1,2,0:T(8,128)}, u32[]{:S(2)}) copy-start(f32[2,512,256]{1,2,0:T(8,128)} %get-tuple-element.54) | copy-start | bytes 3145732
  129.0 2.7 %copy-start = (f32[2,1024,512]{2,1,0:T(8,128)S(1)}, f32[2,1024,512]{2,1,0:T(8,128)}, u32[]{:S(2)}) copy-start(f32[2,1024,512]{2,1,0:T(8,128)} %get-tuple-element.56) | copy-start | bytes 12582916
  131.7 2.1 %copy-start.2 = (f32[2,128,1024]{1,2,0:T(8,128)S(1)}, f32[2,128,1024]{1,2,0:T(8,128)}, u32[]{:S(2)}) copy-start(f32[2,128,1024]{1,2,0:T(8,128)} %get-tuple-element.40) | copy-start | bytes 3145732
  132.5 1.5 copy-start.10
  132.5 2.2 %copy-start.5 = (f32[2,128,640]{2,1,0:T(8,128)S(1)}, f32[2,128,640]{2,1,0:T(8,128)}, u32[]{:S(2)}) copy-start(f32[2,128,640]{2,1,0:T(8,128)} %copy-done.4) | copy-start | bytes 1966084
  132.5 2.2 %copy-start.8 = (bf16[640,256]{1,0:T(8,128)(2,1)S(1)}, bf16[640,256]{1,0:T(8,128)(2,1)}, u32[]{:S(2)}) copy-start(bf16[640,256]{1,0:T(8,128)(2,1)} %param.7) | copy-start | bytes 983044
  148.2 6.6 %copy-start.1 = (f32[2,1024,512]{2,1,0:T(8,128)S(1)}, f32[2,1024,512]{2,1,0:T(8,128)}, u32[]{:S(2)}) copy-start(f32[2,1024,512]{2,1,0:T(8,128)} %get-tuple-element.56) | copy-start | bytes 12582916
  154.8 1.3 copy-start.11
  154.8 1.3 copy-start.12
  154.9 1.3 copy-start.13
  154.9 1.5 copy-start.14
  154.9 1.6 copy-start.22
  154.9 1.6 copy-start.24
  154.9 1.6 copy-start.25
  154.9 1.6 copy-start.26
  154.9 1.6 copy-start.27
  154.9 1.6 copy-start.28
  156.5 2.7 %copy-start.17 = (f32[2,128,128]{2,1,0:T(8,128)S(1)}, f32[2,128,128]{2,1,0:T(8,128)}, u32[]{:S(2)}) copy-start(f32[2,128,128]{2,1,0:T(8,128)} %fusion.129) | copy-start | bytes 393220
  156.6 2.7 %copy-start.18 = (f32[2,128,128]{2,1,0:T(8,128)S(1)}, f32[2,128,128]{2,1,0:T(8,128)}, u32[]{:S(2)}) copy-start(f32[2,128,128]{2,1,0:T(8,128)} %fusion.131) | copy-start | bytes 393220
  156.6 2.7 %copy-start.19 = (f32[2,128,128]{2,1,0:T(8,128)S(1)}, f32[2,128,128]{2,1,0:T(8,128)}, u32[]{:S(2)}) copy-start(f32[2,128,128]{2,1,0:T(8,128)} %fusion.133) | copy-start | bytes 393220
  156.6 2.7 %copy-start.20 = (f32[2,128,128]{2,1,0:T(8,128)S(1)}, f32[2,128,128]{2,1,0:T(8,128)}, u32[]{:S(2)}) copy-start(f32[2,128,128]{2,1,0:T(8,128)} %fusion.135) | copy-start | bytes 393220
  156.6 2.7 %copy-start.21 = (f32[2,128,128]{2,1,0:T(8,128)S(1)}, f32[2,128,128]{2,1,0:T(8,128)}, u32[]{:S(2)}) copy-start(f32[2,128,128]{2,1,0:T(8,128)} %fusion.93) | copy-start | bytes 393220
  156.6 2.7 %copy-start.30 = (f32[2,128]{1,0:T(2,128)S(1)}, f32[2,128]{1,0:T(2,128)}, u32[]{:S(2)}) copy-start(f32[2,128]{1,0:T(2,128)} %copy-done.29) | copy-start | bytes 3076
  156.6 2.7 %copy-start.36 = (f32[2,128]{1,0:T(2,128)S(1)}, f32[2,128]{1,0:T(2,128)}, u32[]{:S(2)}) copy-start(f32[2,128]{1,0:T(2,128)} %get-tuple-element.22) | copy-start | bytes 3076
  156.6 2.7 %copy-start.37 = (f32[2,128]{1,0:T(2,128)S(1)}, f32[2,128]{1,0:T(2,128)}, u32[]{:S(2)}) copy-start(f32[2,128]{1,0:T(2,128)} %get-tuple-element.23) | copy-start | bytes 3076
  156.6 2.7 %copy-start.38 = (f32[2,128]{1,0:T(2,128)S(1)}, f32[2,128]{1,0:T(2,128)}, u32[]{:S(2)}) copy-start(f32[2,128]{1,0:T(2,128)} %get-tuple-element.24) | copy-start | bytes 3076
  156.6 2.7 %copy-start.39 = (f32[2,128]{1,0:T(2,128)S(1)}, f32[2,128]{1,0:T(2,128)}, u32[]{:S(2)}) copy-start(f32[2,128]{1,0:T(2,128)} %get-tuple-element.25) | copy-start | bytes 3076
  156.6 2.7 %copy-start.40 = (f32[2,128]{1,0:T(2,128)S(1)}, f32[2,128]{1,0:T(2,128)}, u32[]{:S(2)}) copy-start(f32[2,128]{1,0:T(2,128)} %get-tuple-element.26) | copy-start | bytes 3076
  156.7 2.7 %copy-start.41 = (f32[2,128]{1,0:T(2,128)S(1)}, f32[2,128]{1,0:T(2,128)}, u32[]{:S(2)}) copy-start(f32[2,128]{1,0:T(2,128)} %get-tuple-element.27) | copy-start | bytes 3076
  156.7 4.0 %copy-start.23 = (f32[2,640]{1,0:T(2,128)S(1)}, f32[2,640]{1,0:T(2,128)}, u32[]{:S(2)}) copy-start(f32[2,640]{1,0:T(2,128)} %pad_maximum_fusion) | copy-start | bytes 15364
